TPU v7x, 128 devices: a whole 4x4x4 slice. The times are simulated.
128 devices in a mesh: tok: 8 (over x, core), head: 8 (over y, z_hi), seq: 2 (over z_lo).
Axes of the slice: x: 4, y: 4, z: 4 (z_hi: 2, z_lo: 2; z = z_hi * 2 + z_lo), core: 2. Of those that a mesh axis runs over, the one named last changes fastest.
Arguments:
- queries: bfloat16 [2, 8192, 4096], P('seq', ('tok', 'head')), may hold values from -6 to 6
- keys: bfloat16 [2, 8192, 4096], P('seq', ('tok', 'head')), may hold values from -6 to 6
- values: bfloat16 [2, 8192, 4096], P('seq', ('tok', 'head')), may hold values from -6 to 6
- rates: float32 [2, 8, 8192], P('seq', 'head', 'tok'), may hold values from 0.00011048543 to 0.0011048544
- fast_one: float32 [8, 512, 512], P('head'), may hold values from -0.25 to 0.25
- fast_two: float32 [8, 512, 512], P('head'), may hold values from -0.25 to 0.25
- fast_three: float32 [8, 512, 512], P('head'), may hold values from -0.25 to 0.25
- grad_out: bfloat16 [2, 8192, 4096], P('seq', ('tok', 'head')), may hold values from -6 to 6
Outputs:
- grad_queries: bfloat16 [2, 8192, 4096], P('seq', ('tok', 'head'))
- grad_keys: bfloat16 [2, 8192, 4096], P('seq', ('tok', 'head'))
- grad_values: bfloat16 [2, 8192, 4096], P('seq', ('tok', 'head'))
- grad_rates: float32 [2, 8, 8192], P('seq', 'head', 'tok')
- grad_fast_one: float32 [8, 512, 512], P('head')
- grad_fast_two: float32 [8, 512, 512], P('head')
- grad_fast_three: float32 [8, 512, 512], P('head')
All inputs are finite; a program needn't handle non-finite values.
Results may differ from a plain program's by a relative error of at most 0.016.
Values may be sent and summed in bfloat16 or wider, within the bound.
A program may use at most 128 MiB of HBM per device.

v0:
```python
import jax
import jax.numpy as jnp
from jax import lax
from jax.sharding import PartitionSpec as P

epsilon = 1e-06


def side_by_side(arrays, axis, split_dim, concat_dim, along):
    ends, at = ([], 0)
    for a in arrays[:-1]:
        at += a.shape[along]
        ends.append(at)
    both = jnp.concatenate(arrays, axis=along)
    return tuple(
        jnp.split(
            lax.all_to_all(both, axis, split_axis=split_dim, concat_axis=concat_dim, tiled=True),
            ends,
            axis=along,
        )
    )


def shortened(value):

    def short(part):
        return part.astype(jnp.bfloat16) if part.dtype == jnp.float32 else part

    return jax.tree.map(short, value)


def matmul(left, right):
    return jnp.dot(
        left.astype(jnp.bfloat16), right.astype(jnp.bfloat16), preferred_element_type=jnp.float32
    )


def matmul_tn(left, right):
    return lax.dot_general(
        left.astype(jnp.bfloat16),
        right.astype(jnp.bfloat16),
        (((0,), (0,)), ((), ())),
        preferred_element_type=jnp.float32,
    )


def matmul_nt(left, right):
    return lax.dot_general(
        left.astype(jnp.bfloat16),
        right.astype(jnp.bfloat16),
        (((1,), (1,)), ((), ())),
        preferred_element_type=jnp.float32,
    )


def activation(preact):
    squash = jax.nn.sigmoid(preact)
    swished = preact * squash
    slope_one = squash * (1.0 + preact * (1.0 - squash))
    slope_two = squash * (1.0 - squash) * (2.0 + preact * (1.0 - 2.0 * squash))
    return (squash, swished, slope_one, slope_two)


def inner_forward(keys_h, values_h, rate_h, w_one, w_two, w_three):
    pre_one = matmul(keys_h, w_one)
    pre_three = matmul(keys_h, w_three)
    parts = activation(pre_one)
    swished, slope_one = (parts[1], parts[2])
    hidden = swished * pre_three
    target = -rate_h[:, None] * values_h.astype(jnp.float32)
    grad_two = matmul_tn(hidden, target)
    back_hidden = matmul_nt(target, w_two)
    delta_one = back_hidden * pre_three * slope_one
    delta_three = back_hidden * swished
    grad_one = matmul_tn(keys_h, delta_one)
    grad_three = matmul_tn(keys_h, delta_three)
    saved = (pre_one, pre_three, target, back_hidden, delta_one, delta_three)
    return ((grad_one, grad_two, grad_three), saved)


def normalize(weight, update):
    ref_norm = jnp.sqrt(jnp.sum(weight * weight, axis=-2, keepdims=True) + epsilon)
    upd_norm = jnp.sqrt(jnp.sum(update * update, axis=-2, keepdims=True) + epsilon)
    return (update * (ref_norm / upd_norm), ref_norm, upd_norm)


def apply_backward(queries_h, cotangent, new_one, new_two, new_three):
    pre_one = matmul(queries_h, new_one)
    pre_three = matmul(queries_h, new_three)
    parts = activation(pre_one)
    swished, slope_one = (parts[1], parts[2])
    hidden = swished * pre_three
    grad_two = matmul_tn(hidden, cotangent)
    back_hidden = matmul_nt(cotangent, new_two)
    delta_one = back_hidden * pre_three * slope_one
    delta_three = back_hidden * swished
    grad_one = matmul_tn(queries_h, delta_one)
    grad_three = matmul_tn(queries_h, delta_three)
    grad_queries = matmul_nt(delta_one, new_one) + matmul_nt(delta_three, new_three)
    return ((grad_one, grad_two, grad_three), grad_queries)


def adjoint(weight, update, ref_norm, upd_norm, grad_new):
    moment = jnp.sum(grad_new * update, axis=-2, keepdims=True)
    factor = ref_norm / upd_norm
    grad_update = factor * grad_new - update * (factor * moment / (upd_norm * upd_norm))
    direct = weight * (moment / (upd_norm * ref_norm)) + grad_update
    return (-grad_update, direct)


def double_backward(
    keys_h, values_h, rate_h, w_one, w_two, w_three, saved, cot_one, cot_two, cot_three
):
    pre_one, pre_three, target, back_hidden, delta_one, delta_three = saved
    parts = activation(pre_one)
    swished, slope_one, slope_two = (parts[1], parts[2], parts[3])
    hidden = swished * pre_three
    grad_hidden = matmul_nt(target, cot_two)
    grad_target = matmul(hidden, cot_two)
    grad_delta_one = matmul(keys_h, cot_one)
    grad_delta_three = matmul(keys_h, cot_three)
    grad_keys = matmul_nt(delta_one, cot_one) + matmul_nt(delta_three, cot_three)
    grad_back = grad_delta_one * pre_three * slope_one + grad_delta_three * swished
    grad_pre_three = grad_delta_one * back_hidden * slope_one + grad_hidden * swished
    grad_pre_one = (
        grad_delta_one * back_hidden * pre_three * slope_two
        + grad_delta_three * back_hidden * slope_one
        + grad_hidden * pre_three * slope_one
    )
    grad_target = grad_target + matmul(grad_back, w_two)
    weight_two = matmul_tn(grad_back, target)
    grad_keys = grad_keys + (matmul_nt(grad_pre_one, w_one) + matmul_nt(grad_pre_three, w_three))
    weight_one = matmul_tn(keys_h, grad_pre_one)
    weight_three = matmul_tn(keys_h, grad_pre_three)
    grad_values = -rate_h[:, None] * grad_target
    grad_rate = -jnp.sum(values_h.astype(jnp.float32) * grad_target, axis=1)
    return (grad_keys, grad_values, grad_rate, (weight_one, weight_two, weight_three))


def body(queries, keys, values, rates, fast_one, fast_two, fast_three, grad_out):
    heads = fast_one.shape[0]
    width = fast_one.shape[1]
    weights = (fast_one, fast_two, fast_three)
    key_local, value_local = side_by_side((keys, values), "head", 2, 1, 0)
    inner_list, saved_list = ([], [])
    head_idx = 0
    start = head_idx * width
    inner, saved = inner_forward(
        key_local[0, :, start : start + width],
        value_local[0, :, start : start + width],
        rates[0, head_idx],
        fast_one[head_idx],
        fast_two[head_idx],
        fast_three[head_idx],
    )
    inner_list.append(inner)
    saved_list.append(saved)
    partial_inner = tuple((jnp.stack([inner_list[0][index]]) for index in range(3)))
    summed_inner = lax.psum(partial_inner, "tok")
    query_local, cot_local = side_by_side((queries, grad_out), "head", 2, 1, 0)
    updates = [weights[index] - summed_inner[index] for index in range(3)]
    normed = [normalize(weights[index], updates[index]) for index in range(3)]
    new_list, query_heads = ([], [])
    head_idx = 0
    start = head_idx * width
    grads_new, grad_queries = apply_backward(
        query_local[0, :, start : start + width],
        cot_local[0, :, start : start + width],
        normed[0][0][head_idx],
        normed[1][0][head_idx],
        normed[2][0][head_idx],
    )
    new_list.append(grads_new)
    query_heads.append(grad_queries)
    partial_new = tuple((jnp.stack([new_list[0][index]]) for index in range(3)))
    query_block = query_heads[0].astype(jnp.bfloat16)[None]
    query_back = lax.all_to_all(query_block, "head", split_axis=1, concat_axis=2, tiled=True)
    summed_new = lax.psum(partial_new, "tok")
    keep_flag = (lax.axis_index("tok") == 0).astype(jnp.float32)
    results = [
        adjoint(
            weights[index], updates[index], normed[index][1], normed[index][2], summed_new[index]
        )
        for index in range(3)
    ]
    cotangents = [results[index][0] for index in range(3)]
    directs = [results[index][1] * keep_flag for index in range(3)]
    key_heads, value_heads, rate_heads, extra_list = ([], [], [], [])
    head_idx = 0
    start = head_idx * width
    grad_keys, grad_values, grad_rate, extra = double_backward(
        key_local[0, :, start : start + width],
        value_local[0, :, start : start + width],
        rates[0, head_idx],
        fast_one[head_idx],
        fast_two[head_idx],
        fast_three[head_idx],
        saved_list[head_idx],
        cotangents[0][head_idx],
        cotangents[1][head_idx],
        cotangents[2][head_idx],
    )
    key_heads.append(grad_keys.astype(jnp.bfloat16))
    value_heads.append(grad_values.astype(jnp.bfloat16))
    rate_heads.append(grad_rate)
    extra_list.append(extra)
    partial_weights = tuple(
        (directs[index] + jnp.stack([extra_list[0][index]]) for index in range(3))
    )
    total_one, total_two, total_three = jax.tree.map(
        lambda part: part.astype(jnp.float32), lax.psum(shortened(partial_weights), ("tok", "seq"))
    )
    key_block = key_heads[0][None]
    value_block = value_heads[0][None]
    key_back, value_back = side_by_side((key_block, value_block), "head", 1, 2, 0)
    rate_grads = jnp.stack(rate_heads)[None]
    return (query_back, key_back, value_back, rate_grads, total_one, total_two, total_three)


def solution(mesh):
    placed = (
        P("seq", ("tok", "head"), None),
        P("seq", ("tok", "head"), None),
        P("seq", ("tok", "head"), None),
        P("seq", "head", "tok"),
        P("head", None, None),
        P("head", None, None),
        P("head", None, None),
        P("seq", ("tok", "head"), None),
    )
    return jax.shard_map(
        body,
        mesh=mesh,
        in_specs=placed,
        out_specs=(
            P("seq", ("tok", "head"), None),
            P("seq", ("tok", "head"), None),
            P("seq", ("tok", "head"), None),
            P("seq", "head", "tok"),
            P("head", None, None),
            P("head", None, None),
            P("head", None, None),
        ),
        check_vma=False,
    )
```

profile of v0, /device:TPU:1, one launch (start us, length us, event | category | flops | bytes accessed | tf_op | source)
XLA Modules:
  0.0 484.2 jit_solution(5529471393245594606)
XLA Ops:
  7.2 1.7 pad_maximum_fusion.1
  8.9 3.8 copy.86
  12.7 8.5 %all-to-all-start.1 = ((bf16[2,128,4096]{1,0,2:T(2,128)(2,1)}), bf16[2,128,4096]{1,0,2:T(2,128)(2,1)}, u32[]{:S(2)}, u32[]{:S(2)}) async-start(bf16[2,128,4096]{1,0,2:T(2,128)(2,1)} %copy.86), calls=%async_computation.1 | async-start | bytes 4194304 | tf_op jit(solution)/shard_map/all_to_all | solution.py:17
  21.2 2.8 copy.82
  24.0 5.5 %copy.83 = bf16[1,128,4096]{1,0,2:T(2,128)(2,1)} copy(bf16[1,128,4096]{2,1,0:T(8,128)(2,1)} %param.15) | data formatting | bytes 2097152 | tf_op args[7]
  29.5 6.4 %pad_maximum_fusion = bf16[2,128,4096]{1,0,2:T(2,128)(2,1)} fusion(bf16[1,128,4096]{1,0,2:T(2,128)(2,1)} %copy.83, bf16[1,128,4096]{1,0,2:T(2,128)(2,1)S(1)} %copy.82), kind=kLoop, calls=%fused_computation.9 | loop fusion | flops 4194304 | bytes 4194304 | tf_op jit(solution)/shard_map/concatenate | solution.py:14
  35.9 15.9 %all-to-all-done.1 = bf16[2,128,4096]{1,0,2:T(2,128)(2,1)} async-done(((bf16[2,128,4096]{1,0,2:T(2,128)(2,1)}), bf16[2,128,4096]{1,0,2:T(2,128)(2,1)}, u32[]{:S(2)}, u32[]{:S(2)}) %all-to-all-start.1) | async-done | bytes 2097184 | tf_op jit(solution)/shard_map/all_to_all | solution.py:17
  51.9 4.4 all-to-all-start
  56.3 4.7 copy.87
  61.1 1.9 copy-done.2
  65.6 1.4 copy-done.13
  66.9 3.1 multiply_convert_fusion.5
  70.1 1.7 convolution_bitcast_fusion.6
  72.1 1.0 copy-done.16
  73.1 1.7 convolution_bitcast_fusion.8
  74.9 11.2 %all-to-all-done = bf16[2,128,4096]{1,0,2:T(2,128)(2,1)} async-done(((bf16[2,128,4096]{1,0,2:T(2,128)(2,1)}), bf16[2,128,4096]{1,0,2:T(2,128)(2,1)}, u32[]{:S(2)}, u32[]{:S(2)}) %all-to-all-start) | async-done | bytes 2097184 | tf_op jit(solution)/shard_map/all_to_all | solution.py:17
  86.0 1.9 copy.84
  88.1 1.3 copy.88
  89.4 1.3 copy.85
  90.7 3.0 convolution_bitcast_fusion.7
  93.7 47.7 %all-reduce.13.cloned.1.call-done = (f32[1,512,512]{2,1,0:T(8,128)}, f32[1,512,512]{2,1,0:T(8,128)}) async-done(((f32[1,512,512]{2,1,0:T(8,128)}, f32[1,512,512]{2,1,0:T(8,128)}), (f32[1,512,512]{2,1,0:T(8,128)}, f32[1,512,512]{2,1,0:T(8,128)})) %all-reduce.13.cloned.1.call-update) | async-done | bytes 2097168 | tf_op jit(solution)/shard_map/psum | solution.py:159
  141.4 2.5 multiply_reduce_fusion.3
  145.5 2.3 multiply_convert_fusion.2
  147.8 1.0 copy-done.34
  148.8 1.7 convolution_bitcast_fusion.4
  151.1 65.1 %all-reduce.11.cloned.1.call-done = (f32[1,512,512]{2,1,0:T(8,128)}, f32[1,512,512]{2,1,0:T(8,128)}) async-done(((f32[1,512,512]{2,1,0:T(8,128)}, f32[1,512,512]{2,1,0:T(8,128)}), (f32[1,512,512]{2,1,0:T(8,128)}, f32[1,512,512]{2,1,0:T(8,128)})) %all-reduce.11.cloned.1.call-update) | async-done | bytes 2097168 | tf_op jit(solution)/shard_map/psum | solution.py:159
  216.1 2.4 multiply_reduce_fusion.1
  219.0 2.8 multiply_convert_fusion.3
  221.8 1.7 convolution_bitcast_fusion.5
  223.5 2.1 fusion.47
  225.6 1.8 convolution_bitcast_fusion.3
  227.5 2.7 fusion.12
  230.1 3.0 copy.101
  233.6 9.0 %reduce.9 = bf16[1024,512]{1,0:T(8,128)(2,1)} reduce(bf16[1024,1,512]{2,1,0:T(2,128)(2,1)} %bitcast.164, bf16[]{:T(256)} %broadcast.129), dimensions={1}, to_apply=%bitcast.149.reduce_sub_computation | reduce | bytes 2097154
  242.6 2.8 reshape.255
  245.4 6.6 %all-to-all-start.2 = ((bf16[8,2,32768]{2,1,0:T(2,128)(2,1)}), bf16[8,2,32768]{2,1,0:T(2,128)(2,1)}, u32[]{:S(2)}, u32[]{:S(2)}) async-start(bf16[8,2,32768]{2,1,0:T(2,128)(2,1)} %reshape.255), calls=%async_computation.2 | async-start | bytes 2097152 | tf_op jit(solution)/shard_map/all_to_all | solution.py:177
  252.0 1.5 fusion.27
  253.6 2.1 fusion.62
  255.6 2.1 fusion.60
  257.7 35.6 %all-reduce.9.cloned.1.call-done = (f32[1,512,512]{2,1,0:T(8,128)}, f32[1,512,512]{2,1,0:T(8,128)}) async-done(((f32[1,512,512]{2,1,0:T(8,128)}, f32[1,512,512]{2,1,0:T(8,128)}), (f32[1,512,512]{2,1,0:T(8,128)}, f32[1,512,512]{2,1,0:T(8,128)})) %all-reduce.9.cloned.1.call-update) | async-done | bytes 2097168 | tf_op jit(solution)/shard_map/psum | solution.py:178
  293.3 1.5 multiply_reduce_fusion.2
  296.3 0.7 fusion.59
  300.7 0.8 copy-done.21
  301.6 2.7 add_convert_fusion.2
  304.3 0.7 fusion.35
  305.3 1.0 copy-done.1
  306.6 0.9 fusion.9
  308.5 0.9 fusion.13
  309.6 3.5 copy.93
  313.2 1.6 fusion.17
  314.8 1.6 fusion.18
  316.4 6.7 %all-to-all-start.3 = ((bf16[2,1024,512]{2,0,1:T(2,128)(2,1)}), bf16[2,1024,512]{2,0,1:T(2,128)(2,1)}, u32[]{:S(2)}, u32[]{:S(2)}) async-start(bf16[2,1024,512]{2,0,1:T(2,128)(2,1)} %copy.93), calls=%async_computation.3 | async-start | bytes 4194304 | tf_op jit(solution)/shard_map/all_to_all | solution.py:17
  323.2 3.1 fusion.19
  326.4 4.5 reshape.256
  331.9 1.3 copy.96
  333.8 127.8 %all-reduce.15.cloned.1.call-done = (bf16[1,512,512]{2,1,0:T(8,128)(2,1)}, bf16[1,512,512]{2,1,0:T(8,128)(2,1)}, bf16[1,512,512]{2,1,0:T(8,128)(2,1)}) async-done(((bf16[1,512,512]{2,1,0:T(8,128)(2,1)}, bf16[1,512,512]{2,1,0:T(8,128)(2,1)}, bf16[1,512,512]{2,1,0:T(8,128)(2,1)}), (bf16[1,512,512]{2,1,0:T(8,128)(2,1)}, bf16[1,512,512]{2,1,0:T(8,128)(2,1)}, ...) | async-done | bytes 1572880 | tf_op jit(solution)/shard_map/psum | solution.py:211
  461.6 2.2 convert_element_type.196
  463.8 2.1 convert_element_type.198
  466.0 1.1 convert_element_type.200
  467.1 5.5 %fusion.55 = (bf16[1,128,8,512]{3,0,1,2:T(2,128)(2,1)S(1)}, bf16[1,128,8,512]{3,0,1,2:T(2,128)(2,1)S(1)}) fusion(bf16[2,128,8,512]{3,0,1,2:T(2,128)(2,1)} %bitcast.33), kind=kLoop, calls=%fused_computation.110 | loop fusion | bytes 4194304 | tf_op jit(solution)/shard_map/split | solution.py:16
  472.6 1.1 copy.94
  473.7 1.3 split.27
  475.0 1.1 copy.95
  476.2 1.3 split.29
  (111 shorter events, 14.7 us)
Async XLA Ops:
  12.7 8.5 %copy-start.40 = (f32[1,1,1024]{2,1,0:T(1,128)S(1)}, f32[1,1,1024]{2,1,0:T(1,128)}, u32[]{:S(2)}) copy-start(f32[1,1,1024]{2,1,0:T(1,128)} %param.11) | copy-start | bytes 12292
  12.7 8.5 %copy-start.28 = (bf16[1,128,4096]{2,1,0:T(8,128)(2,1)S(1)}, bf16[1,128,4096]{2,1,0:T(8,128)(2,1)}, u32[]{:S(2)}) copy-start(bf16[1,128,4096]{2,1,0:T(8,128)(2,1)} %param.8) | copy-start | bytes 3145732
  12.7 39.2 %all-to-all-start.1 = ((bf16[2,128,4096]{1,0,2:T(2,128)(2,1)}), bf16[2,128,4096]{1,0,2:T(2,128)(2,1)}, u32[]{:S(2)}, u32[]{:S(2)}) async-start(bf16[2,128,4096]{1,0,2:T(2,128)(2,1)} %copy.86), calls=%async_computation.1 | async-start | bytes 4194304 | tf_op jit(solution)/shard_map/all_to_all | solution.py:17
  51.9 34.2 %all-to-all-start = ((bf16[2,128,4096]{1,0,2:T(2,128)(2,1)}), bf16[2,128,4096]{1,0,2:T(2,128)(2,1)}, u32[]{:S(2)}, u32[]{:S(2)}) async-start(bf16[2,128,4096]{1,0,2:T(2,128)(2,1)} %pad_maximum_fusion), calls=%async_computation | async-start | bytes 4194304 | tf_op jit(solution)/shard_map/all_to_all | solution.py:17
  56.2 85.2 %all-reduce.13.cloned.1.call-start = ((), (), s32[]{:S(2)}) async-start(), calls=%async_computation.6 | async-start | bytes 4194304 | tf_op jit(solution)/shard_map/psum | solution.py:159
  61.0 10.8 %copy-start = (bf16[2,128,8,512]{3,1,2,0:T(8,128)(2,1)}, bf16[2,128,8,512]{3,1,2,0:T(8,128)(2,1)S(1)}, u32[]{:S(2)}) copy-start(bf16[2,128,8,512]{3,1,2,0:T(8,128)(2,1)S(1)} %copy.87) | copy-start | bytes 6291460
  61.0 2.0 copy-start.2
  63.0 1.2 copy-start.6
  64.2 1.4 copy-start.22
  64.9 5.2 %copy-start.24 = (f32[1024,512]{1,0:T(8,128)}, f32[1024,512]{1,0:T(8,128)S(1)}, u32[]{:S(2)}) copy-start(f32[1024,512]{1,0:T(8,128)S(1)} %fusion.37) | copy-start | bytes 6291460
  64.9 2.0 copy-start.13
  65.3 4.8 copy-start.35
  70.1 1.7 copy-start.31
  70.1 2.0 copy-start.29
  72.1 1.0 copy-start.16
  74.8 141.3 %all-reduce.11.cloned.1.call-start = ((), (), s32[]{:S(2)}) async-start(), calls=%async_computation.5 | async-start | bytes 4194304 | tf_op jit(solution)/shard_map/psum | solution.py:159
  90.7 50.8 %copy-start.7 = (f32[1,512,512]{2,1,0:T(8,128)S(1)}, f32[1,512,512]{2,1,0:T(8,128)}, u32[]{:S(2)}) copy-start(f32[1,512,512]{2,1,0:T(8,128)} %param.12) | copy-start | bytes 3145732
  141.4 2.5 copy-start.19
  143.9 1.0 copy-start.4
  144.0 1.6 copy-start.37
  144.7 3.1 copy-start.26
  147.8 1.0 copy-start.34
  150.5 142.7 %all-reduce.9.cloned.1.call-start = ((), (), s32[]{:S(2)}) async-start(), calls=%async_computation.4 | async-start | bytes 4194304 | tf_op jit(solution)/shard_map/psum | solution.py:178
  216.1 2.4 copy-start.20
  216.1 2.9 copy-start.27
  223.5 2.1 copy-start.38
  245.4 71.0 %all-to-all-start.2 = ((bf16[8,2,32768]{2,1,0:T(2,128)(2,1)}), bf16[8,2,32768]{2,1,0:T(2,128)(2,1)}, u32[]{:S(2)}, u32[]{:S(2)}) async-start(bf16[8,2,32768]{2,1,0:T(2,128)(2,1)} %reshape.255), calls=%async_computation.2 | async-start | bytes 2097152 | tf_op jit(solution)/shard_map/all_to_all | solution.py:177
  253.5 2.1 copy-start.33
  293.3 1.5 copy-start.11
  295.1 1.2 copy-start.32
  295.1 4.7 copy-start.41
  296.3 1.2 copy-start.5
  296.3 1.5 copy-start.12
  297.9 1.2 copy-start.30
  297.9 1.9 copy-start.36
  298.2 1.9 copy-start.23
  298.2 2.5 copy-start.25
  299.1 2.5 copy-start.21
  301.6 2.7 copy-start.8
  304.3 1.0 copy-start.18
  304.3 2.0 copy-start.1
  304.3 2.2 copy-start.14
  306.6 1.2 copy-start.3
  306.6 1.9 copy-start.15
  309.6 3.5 copy-start.10
  313.2 1.7 copy-start.17
  316.4 6.8 %copy-start.9 = (f32[1,512,512]{2,1,0:T(8,128)S(1)}, f32[1,512,512]{2,1,0:T(8,128)}, u32[]{:S(2)}) copy-start(f32[1,512,512]{2,1,0:T(8,128)} %param.12) | copy-start | bytes 3145732
  316.4 150.6 %all-to-all-start.3 = ((bf16[2,1024,512]{2,0,1:T(2,128)(2,1)}), bf16[2,1024,512]{2,0,1:T(2,128)(2,1)}, u32[]{:S(2)}, u32[]{:S(2)}) async-start(bf16[2,1024,512]{2,0,1:T(2,128)(2,1)} %copy.93), calls=%async_computation.3 | async-start | bytes 4194304 | tf_op jit(solution)/shard_map/all_to_all | solution.py:17
  323.2 138.4 %all-reduce.15.cloned.1.call-start = ((), (), s32[]{:S(2)}) async-start(), calls=%async_computation.7 | async-start | bytes 3145728 | tf_op jit(solution)/shard_map/psum | solution.py:211
  461.6 4.4 copy-start.39
Sparse Core Ops, SparseCore 0:
  74.9 66.4 all-reduce.12
  150.7 65.4 all-reduce.10
  227.6 65.6 all-reduce.8
  326.9 134.6 all-reduce.14
where the time goes:
time: 493 us; the launch traced here: 484 us
  waiting for transfers between devices  303 us (61%)
  local copies, waits for them, and re-layouts  62.1 us (13%)
  matrix products  44.9 us (9%)
  other arithmetic  32.7 us (7%)
  starting transfers between devices  26.8 us (5%)
  between operations  14.5 us (3%)
    psum x1, waiting for transfers between devices, body(): lax.psum(shortened(partial_weights), ('tok', 'seq'))  128 us
    psum x2, waiting for transfers between devices, body(): summed_inner = lax.psum(partial_inner, 'tok')  113 us
    psum x1, waiting for transfers between devices, body(): summed_new = lax.psum(partial_new, 'tok')  35.6 us
    unnamed x91, local copies, waits for them, and re-layouts  31.3 us
    all_to_all x3, waiting for transfers between devices, side_by_side(): lax.all_to_all(both, axis, split_axis=split_dim, concat_axis=concat_dim,...  27.1 us
    all_to_all x3, starting transfers between devices, side_by_side(): lax.all_to_all(both, axis, split_axis=split_dim, concat_axis=concat_dim,...  19.5 us
    dot_general x9, matrix products, matmul_tn(): lax.dot_general(left.astype(jnp.bfloat16), right.astype(jnp.bfloat16), ((...  18.1 us
    dot_general x9, matrix products, matmul_nt(): lax.dot_general(left.astype(jnp.bfloat16), right.astype(jnp.bfloat16), ((...  17.5 us
  transfers between devices with their start and end apart: 8, of which 6 were waited for; matrix products, arithmetic and copies ran while one was open for 19% of the time, Pallas kernels for 0%

commit v1 on v0

--- a/solution.py
+++ b/solution.py
@@ -4,6 +4,11 @@
 from jax.sharding import PartitionSpec as P
 
 epsilon = 1e-06
+
+
+def by_each_axis(value_2, axis_one, axis_two):
+    half = lax.psum(value_2, axis_one)
+    return lax.psum(half, axis_two)
 
 
 def side_by_side(arrays, axis, split_dim, concat_dim, along):
@@ -208,7 +213,8 @@
         (directs[index] + jnp.stack([extra_list[0][index]]) for index in range(3))
     )
     total_one, total_two, total_three = jax.tree.map(
-        lambda part: part.astype(jnp.float32), lax.psum(shortened(partial_weights), ("tok", "seq"))
+        lambda part: part.astype(jnp.float32),
+        by_each_axis(shortened(partial_weights), "tok", "seq"),
     )
     key_block = key_heads[0][None]
     value_block = value_heads[0][None]

time: 493 us -> 475 us (0.963)
  waiting for transfers between devices: 303 us -> 284 us
    psum x1 -> x2, waiting for transfers between devices: 128 us -> 109 us  [the longest x1 64.3 us: by_each_axis(): half = lax.psum(value_2, axis_one)]
    unnamed x91 -> x97, local copies, waits for them, and re-layouts: 31.3 us -> 31.7 us
  transfers between devices with their start and end apart: 8 -> 9, of which waited for: 6 -> 7; matrix products, arithmetic and copies ran while one was open for 19% -> 21% of each run, Pallas kernels for 0% -> 0%
where the time goes in v1:
time: 475 us; the launch traced here: 466 us
  waiting for transfers between devices  284 us (60%)
  local copies, waits for them, and re-layouts  62.6 us (13%)
  matrix products  45.5 us (10%)
  other arithmetic  32.7 us (7%)
  starting transfers between devices  26.8 us (6%)
  between operations  14.5 us (3%)
    psum x2, waiting for transfers between devices, body(): summed_inner = lax.psum(partial_inner, 'tok')  113 us
    psum x1, waiting for transfers between devices, by_each_axis(): half = lax.psum(value_2, axis_one)  64.3 us
    psum x1, waiting for transfers between devices, by_each_axis(): return lax.psum(half, axis_two)  44.2 us
    psum x1, waiting for transfers between devices, body(): summed_new = lax.psum(partial_new, 'tok')  35.6 us
    unnamed x97, local copies, waits for them, and re-layouts  31.7 us
    all_to_all x3, waiting for transfers between devices, side_by_side(): lax.all_to_all(both, axis, split_axis=split_dim, concat_axis=concat_dim,...  27.1 us
    all_to_all x3, starting transfers between devices, side_by_side(): lax.all_to_all(both, axis, split_axis=split_dim, concat_axis=concat_dim,...  19.6 us
    dot_general x9, matrix products, matmul_tn(): lax.dot_general(left.astype(jnp.bfloat16), right.astype(jnp.bfloat16), ((...  18.9 us
  transfers between devices with their start and end apart: 9, of which 7 were waited for; matrix products, arithmetic and copies ran while one was open for 21% of the time, Pallas kernels for 0%

profile of v1, /device:TPU:1, one launch (start us, length us, event | category | flops | bytes accessed | tf_op | source)
XLA Modules:
  0.0 466.1 jit_solution(16336467388483317776)
XLA Ops:
  7.2 1.7 pad_maximum_fusion.1
  8.9 3.8 copy.86
  12.7 8.5 %all-to-all-start.1 = ((bf16[2,128,4096]{1,0,2:T(2,128)(2,1)}), bf16[2,128,4096]{1,0,2:T(2,128)(2,1)}, u32[]{:S(2)}, u32[]{:S(2)}) async-start(bf16[2,128,4096]{1,0,2:T(2,128)(2,1)} %copy.86), calls=%async_computation.1 | async-start | bytes 4194304 | tf_op jit(solution)/shard_map/all_to_all | solution.py:22
  21.2 2.8 copy.82
  24.0 5.5 %copy.83 = bf16[1,128,4096]{1,0,2:T(2,128)(2,1)} copy(bf16[1,128,4096]{2,1,0:T(8,128)(2,1)} %param.15) | data formatting | bytes 2097152 | tf_op args[7]
  29.5 6.4 %pad_maximum_fusion = bf16[2,128,4096]{1,0,2:T(2,128)(2,1)} fusion(bf16[1,128,4096]{1,0,2:T(2,128)(2,1)} %copy.83, bf16[1,128,4096]{1,0,2:T(2,128)(2,1)S(1)} %copy.82), kind=kLoop, calls=%fused_computation.9 | loop fusion | flops 4194304 | bytes 4194304 | tf_op jit(solution)/shard_map/concatenate | solution.py:19
  35.9 15.9 %all-to-all-done.1 = bf16[2,128,4096]{1,0,2:T(2,128)(2,1)} async-done(((bf16[2,128,4096]{1,0,2:T(2,128)(2,1)}), bf16[2,128,4096]{1,0,2:T(2,128)(2,1)}, u32[]{:S(2)}, u32[]{:S(2)}) %all-to-all-start.1) | async-done | bytes 2097184 | tf_op jit(solution)/shard_map/all_to_all | solution.py:22
  51.9 4.4 all-to-all-start
  56.3 4.7 %copy.87 = bf16[2,128,8,512]{3,1,2,0:T(8,128)(2,1)S(1)} copy(bf16[2,128,8,512]{1,0,3,2:T(2,128)(2,1)} %bitcast.3) | data formatting | bytes 4194304 | tf_op jit(solution)/shard_map/all_to_all | solution.py:22
  61.2 1.9 copy-done.2
  65.6 1.4 copy-done.15
  67.0 3.1 multiply_convert_fusion.5
  70.1 1.7 convolution_bitcast_fusion.6
  72.2 1.0 copy-done.18
  73.1 1.7 convolution_bitcast_fusion.8
  74.9 11.1 %all-to-all-done = bf16[2,128,4096]{1,0,2:T(2,128)(2,1)} async-done(((bf16[2,128,4096]{1,0,2:T(2,128)(2,1)}), bf16[2,128,4096]{1,0,2:T(2,128)(2,1)}, u32[]{:S(2)}, u32[]{:S(2)}) %all-to-all-start) | async-done | bytes 2097184 | tf_op jit(solution)/shard_map/all_to_all | solution.py:22
  86.1 1.9 copy.84
  88.1 1.3 copy.88
  89.4 1.3 copy.85
  90.7 3.0 convolution_bitcast_fusion.7
  93.7 47.6 %all-reduce.15.cloned.1.call-done = (f32[1,512,512]{2,1,0:T(8,128)}, f32[1,512,512]{2,1,0:T(8,128)}) async-done(((f32[1,512,512]{2,1,0:T(8,128)}, f32[1,512,512]{2,1,0:T(8,128)}), (f32[1,512,512]{2,1,0:T(8,128)}, f32[1,512,512]{2,1,0:T(8,128)})) %all-reduce.15.cloned.1.call-update) | async-done | bytes 2097168 | tf_op jit(solution)/shard_map/psum | solution.py:164
  141.4 2.5 multiply_reduce_fusion.3
  145.5 2.3 multiply_convert_fusion.2
  147.8 1.0 copy-done.37
  148.8 1.7 convolution_bitcast_fusion.4
  151.0 65.0 %all-reduce.13.cloned.1.call-done = (f32[1,512,512]{2,1,0:T(8,128)}, f32[1,512,512]{2,1,0:T(8,128)}) async-done(((f32[1,512,512]{2,1,0:T(8,128)}, f32[1,512,512]{2,1,0:T(8,128)}), (f32[1,512,512]{2,1,0:T(8,128)}, f32[1,512,512]{2,1,0:T(8,128)})) %all-reduce.13.cloned.1.call-update) | async-done | bytes 2097168 | tf_op jit(solution)/shard_map/psum | solution.py:164
  216.0 2.4 multiply_reduce_fusion.1
  218.9 2.8 multiply_convert_fusion.3
  221.7 1.7 convolution_bitcast_fusion.5
  223.4 2.1 fusion.47
  225.5 1.8 convolution_bitcast_fusion.3
  227.3 2.7 fusion.12
  230.0 3.0 copy.101
  233.5 9.0 %reduce.9 = bf16[1024,512]{1,0:T(8,128)(2,1)} reduce(bf16[1024,1,512]{2,1,0:T(2,128)(2,1)} %bitcast.164, bf16[]{:T(256)} %broadcast.129), dimensions={1}, to_apply=%bitcast.149.reduce_sub_computation | reduce | bytes 2097154
  242.5 2.8 reshape.255
  245.3 6.6 %all-to-all-start.2 = ((bf16[8,2,32768]{2,1,0:T(2,128)(2,1)}), bf16[8,2,32768]{2,1,0:T(2,128)(2,1)}, u32[]{:S(2)}, u32[]{:S(2)}) async-start(bf16[8,2,32768]{2,1,0:T(2,128)(2,1)} %reshape.255), calls=%async_computation.2 | async-start | bytes 2097152 | tf_op jit(solution)/shard_map/all_to_all | solution.py:182
  251.9 1.5 fusion.27
  253.4 2.1 fusion.62
  255.5 2.1 fusion.60
  257.6 35.6 %all-reduce.11.cloned.1.call-done = (f32[1,512,512]{2,1,0:T(8,128)}, f32[1,512,512]{2,1,0:T(8,128)}) async-done(((f32[1,512,512]{2,1,0:T(8,128)}, f32[1,512,512]{2,1,0:T(8,128)}), (f32[1,512,512]{2,1,0:T(8,128)}, f32[1,512,512]{2,1,0:T(8,128)})) %all-reduce.11.cloned.1.call-update) | async-done | bytes 2097168 | tf_op jit(solution)/shard_map/psum | solution.py:183
  293.1 1.5 multiply_reduce_fusion.2
  300.6 0.8 copy-done.24
  301.4 2.6 add_convert_fusion.2
  304.1 0.7 fusion.35
  305.0 1.0 copy-done.3
  306.8 0.9 fusion.13
  308.6 0.9 fusion.9
  309.8 3.5 copy.93
  313.3 1.6 fusion.17
  314.9 6.7 %all-to-all-start.3 = ((bf16[2,1024,512]{2,0,1:T(2,128)(2,1)}), bf16[2,1024,512]{2,0,1:T(2,128)(2,1)}, u32[]{:S(2)}, u32[]{:S(2)}) async-start(bf16[2,1024,512]{2,0,1:T(2,128)(2,1)} %copy.93), calls=%async_computation.3 | async-start | bytes 4194304 | tf_op jit(solution)/shard_map/all_to_all | solution.py:22
  321.7 3.9 fusion.18
  325.7 1.7 fusion.19
  327.4 64.3 %all-reduce.17.cloned.1.call-done = (bf16[1,512,512]{2,1,0:T(8,128)(2,1)}, bf16[1,512,512]{2,1,0:T(8,128)(2,1)}, bf16[1,512,512]{2,1,0:T(8,128)(2,1)}) async-done(((bf16[1,512,512]{2,1,0:T(8,128)(2,1)}, bf16[1,512,512]{2,1,0:T(8,128)(2,1)}, bf16[1,512,512]{2,1,0:T(8,128)(2,1)}), (bf16[1,512,512]{2,1,0:T(8,128)(2,1)}, bf16[1,512,512]{2,1,0:T(8,128)(2,1)}, ...) | async-done | bytes 1572880 | tf_op jit(solution)/shard_map/psum | solution.py:10
  391.8 4.5 reshape.256
  397.3 1.3 copy.96
  399.2 5.6 %fusion.55 = (bf16[1,128,8,512]{3,0,1,2:T(2,128)(2,1)S(1)}, bf16[1,128,8,512]{3,0,1,2:T(2,128)(2,1)S(1)}) fusion(bf16[2,128,8,512]{3,0,1,2:T(2,128)(2,1)} %bitcast.33), kind=kLoop, calls=%fused_computation.110 | loop fusion | bytes 4194304 | tf_op jit(solution)/shard_map/split | solution.py:21
  404.8 1.1 copy.94
  405.9 1.3 split.27
  407.2 1.1 copy.95
  408.4 1.3 split.29
  409.7 44.2 %all-reduce.19.cloned.1.call-done = (bf16[1,512,512]{2,1,0:T(8,128)(2,1)}, bf16[1,512,512]{2,1,0:T(8,128)(2,1)}, bf16[1,512,512]{2,1,0:T(8,128)(2,1)}) async-done(((bf16[1,512,512]{2,1,0:T(8,128)(2,1)}, bf16[1,512,512]{2,1,0:T(8,128)(2,1)}, bf16[1,512,512]{2,1,0:T(8,128)(2,1)}), (bf16[1,512,512]{2,1,0:T(8,128)(2,1)}, bf16[1,512,512]{2,1,0:T(8,128)(2,1)}, ...) | async-done | bytes 1572880 | tf_op jit(solution)/shard_map/psum | solution.py:11
  453.9 2.2 convert_element_type.196
  456.1 2.1 convert_element_type.198
  458.2 1.1 convert_element_type.200
  (120 shorter events, 15.9 us)
Async XLA Ops:
  12.7 8.5 %copy-start.43 = (f32[1,1,1024]{2,1,0:T(1,128)S(1)}, f32[1,1,1024]{2,1,0:T(1,128)}, u32[]{:S(2)}) copy-start(f32[1,1,1024]{2,1,0:T(1,128)} %param.11) | copy-start | bytes 12292
  12.7 8.5 %copy-start.31 = (bf16[1,128,4096]{2,1,0:T(8,128)(2,1)S(1)}, bf16[1,128,4096]{2,1,0:T(8,128)(2,1)}, u32[]{:S(2)}) copy-start(bf16[1,128,4096]{2,1,0:T(8,128)(2,1)} %param.8) | copy-start | bytes 3145732
  12.7 39.2 %all-to-all-start.1 = ((bf16[2,128,4096]{1,0,2:T(2,128)(2,1)}), bf16[2,128,4096]{1,0,2:T(2,128)(2,1)}, u32[]{:S(2)}, u32[]{:S(2)}) async-start(bf16[2,128,4096]{1,0,2:T(2,128)(2,1)} %copy.86), calls=%async_computation.1 | async-start | bytes 4194304 | tf_op jit(solution)/shard_map/all_to_all | solution.py:22
  51.9 34.2 %all-to-all-start = ((bf16[2,128,4096]{1,0,2:T(2,128)(2,1)}), bf16[2,128,4096]{1,0,2:T(2,128)(2,1)}, u32[]{:S(2)}, u32[]{:S(2)}) async-start(bf16[2,128,4096]{1,0,2:T(2,128)(2,1)} %pad_maximum_fusion), calls=%async_computation | async-start | bytes 4194304 | tf_op jit(solution)/shard_map/all_to_all | solution.py:22
  56.2 85.1 %all-reduce.15.cloned.1.call-start = ((), (), s32[]{:S(2)}) async-start(), calls=%async_computation.6 | async-start | bytes 4194304 | tf_op jit(solution)/shard_map/psum | solution.py:164
  61.0 10.8 %copy-start = (bf16[2,128,8,512]{3,1,2,0:T(8,128)(2,1)}, bf16[2,128,8,512]{3,1,2,0:T(8,128)(2,1)S(1)}, u32[]{:S(2)}) copy-start(bf16[2,128,8,512]{3,1,2,0:T(8,128)(2,1)S(1)} %copy.87) | copy-start | bytes 6291460
  61.0 2.0 copy-start.2
  63.0 1.2 copy-start.7
  64.2 1.4 copy-start.25
  65.0 5.2 %copy-start.27 = (f32[1024,512]{1,0:T(8,128)}, f32[1024,512]{1,0:T(8,128)S(1)}, u32[]{:S(2)}) copy-start(f32[1024,512]{1,0:T(8,128)S(1)} %fusion.37) | copy-start | bytes 6291460
  65.0 2.0 copy-start.15
  65.3 4.8 %copy-start.38 = (bf16[1,8,128,512]{3,2,1,0:T(8,128)(2,1)}, bf16[1,8,128,512]{3,2,1,0:T(8,128)(2,1)S(1)}, u32[]{:S(2)}) copy-start(bf16[1,8,128,512]{3,2,1,0:T(8,128)(2,1)S(1)} %fusion.7) | copy-start | bytes 3145732
  70.1 1.7 copy-start.34
  70.1 2.0 copy-start.32
  72.1 1.0 copy-start.18
  74.9 141.2 %all-reduce.13.cloned.1.call-start = ((), (), s32[]{:S(2)}) async-start(), calls=%async_computation.5 | async-start | bytes 4194304 | tf_op jit(solution)/shard_map/psum | solution.py:164
  90.7 50.7 %copy-start.8 = (f32[1,512,512]{2,1,0:T(8,128)S(1)}, f32[1,512,512]{2,1,0:T(8,128)}, u32[]{:S(2)}) copy-start(f32[1,512,512]{2,1,0:T(8,128)} %param.12) | copy-start | bytes 3145732
  141.4 2.5 copy-start.22
  143.9 1.0 copy-start.4
  143.9 1.6 copy-start.40
  144.6 3.2 copy-start.29
  147.8 1.0 copy-start.37
  150.5 142.6 %all-reduce.11.cloned.1.call-start = ((), (), s32[]{:S(2)}) async-start(), calls=%async_computation.4 | async-start | bytes 4194304 | tf_op jit(solution)/shard_map/psum | solution.py:183
  216.0 2.4 copy-start.23
  216.0 2.9 copy-start.30
  223.4 2.1 copy-start.41
  245.3 69.7 %all-to-all-start.2 = ((bf16[8,2,32768]{2,1,0:T(2,128)(2,1)}), bf16[8,2,32768]{2,1,0:T(2,128)(2,1)}, u32[]{:S(2)}, u32[]{:S(2)}) async-start(bf16[8,2,32768]{2,1,0:T(2,128)(2,1)} %reshape.255), calls=%async_computation.2 | async-start | bytes 2097152 | tf_op jit(solution)/shard_map/all_to_all | solution.py:182
  253.4 2.1 copy-start.36
  293.1 1.5 copy-start.12
  295.0 1.2 copy-start.35
  295.0 4.7 %copy-start.44 = (f32[1024,512]{1,0:T(8,128)S(1)}, f32[1024,512]{1,0:T(8,128)}, u32[]{:S(2)}) copy-start(f32[1024,512]{1,0:T(8,128)} %get-tuple-element.62) | copy-start | bytes 6291460
  296.2 1.2 copy-start.5
  296.2 1.5 copy-start.14
  297.7 1.2 copy-start.33
  297.7 1.9 copy-start.39
  298.0 1.9 copy-start.26
  298.1 2.5 copy-start.28
  298.9 2.5 copy-start.24
  301.4 2.7 copy-start.9
  304.1 1.0 copy-start.19
  304.1 3.6 copy-start.21
  304.1 2.0 copy-start.3
  304.1 2.6 copy-start.17
  306.8 1.6 copy-start.1
  306.8 1.9 copy-start.16
  309.7 3.5 copy-start.11
  314.9 6.8 %copy-start.6 = (f32[1,512,512]{2,1,0:T(8,128)S(1)}, f32[1,512,512]{2,1,0:T(8,128)}, u32[]{:S(2)}) copy-start(f32[1,512,512]{2,1,0:T(8,128)} %copy-done.4) | copy-start | bytes 3145732
  314.9 84.3 %all-to-all-start.3 = ((bf16[2,1024,512]{2,0,1:T(2,128)(2,1)}), bf16[2,1024,512]{2,0,1:T(2,128)(2,1)}, u32[]{:S(2)}, u32[]{:S(2)}) async-start(bf16[2,1024,512]{2,0,1:T(2,128)(2,1)} %copy.93), calls=%async_computation.3 | async-start | bytes 4194304 | tf_op jit(solution)/shard_map/all_to_all | solution.py:22
  321.7 70.1 %all-reduce.17.cloned.1.call-start = ((), (), s32[]{:S(2)}) async-start(), calls=%async_computation.7 | async-start | bytes 3145728 | tf_op jit(solution)/shard_map/psum | solution.py:10
  321.7 4.0 copy-start.10
  321.7 4.0 copy-start.13
  321.7 3.9 copy-start.20
  327.4 126.5 %all-reduce.19.cloned.1.call-start = ((), (), s32[]{:S(2)}) async-start(), calls=%async_computation.8 | async-start | bytes 3145728 | tf_op jit(solution)/shard_map/psum | solution.py:11
  453.9 4.4 copy-start.42
Sparse Core Ops, SparseCore 0:
  75.0 66.3 all-reduce.14
  150.6 65.3 all-reduce.12
  227.4 65.6 all-reduce.10
  327.5 64.2 all-reduce.16
  394.2 59.5 all-reduce.18
